TPU v7x, 256 devices: a whole 4x4x8 slice. The times are simulated.
256 devices in a mesh: ka: 32 (over x, z_lo, core), tr: 2 (over z_hi), tc: 4 (over y).
Axes of the slice: x: 4, y: 4, z: 8 (z_hi: 2, z_lo: 4; z = z_hi * 4 + z_lo), core: 2. Of those that a mesh axis runs over, the one named last changes fastest.
Arguments:
- green_less: float32 [2, 32, 1024, 1024], P(None, 'ka', 'tr', 'tc'), may hold values from -6 to 6
- green_great: float32 [2, 32, 1024, 1024], P(None, 'ka', 'tr', 'tc'), may hold values from -6 to 6
- screened: float32 [2, 32, 1024, 1024], P(None, 'ka', 'tr', 'tc'), may hold values from -6 to 6
Outputs:
- collision: float32 [2, 32, 1024, 1024], P(None, 'ka', 'tr', 'tc')
- green_next: float32 [2, 32, 1024, 1024], P(None, 'ka', 'tr', 'tc')
All inputs are finite; a program needn't handle non-finite values.
Results may differ from a plain program's by a relative error of at most 0.00012.
Values sent between devices are 32-bit elements; how exact they have to be, the bound alone decides.
A program may use at most 64 MiB of HBM per device.

v0:
```python
import math

import jax
import jax.numpy as jnp
from jax import lax
from jax.sharding import PartitionSpec as P

NT = 1024


def angle_tables(points):
    indices = jnp.arange(points, dtype=jnp.int32)
    phases = indices[:, None] * indices[None, :] % points
    angles = phases.astype(jnp.float32) * (2.0 * math.pi / points)
    return (jnp.cos(angles), jnp.sin(angles))


def along_momenta(matrix_in, source):
    return jnp.tensordot(matrix_in, source, axes=1, precision=lax.Precision.HIGHEST)


def to_real(source, cosine_table, sine_table):
    factor = source.shape[1] ** (-0.5)
    real_part = along_momenta(cosine_table, source[0]) - along_momenta(sine_table, source[1])
    imag_part = along_momenta(cosine_table, source[1]) + along_momenta(sine_table, source[0])
    return jnp.stack([real_part, imag_part]) * factor


def to_momentum(source, cosine_table, sine_table):
    factor = source.shape[1] ** (-0.5)
    real_part = along_momenta(cosine_table, source[0]) + along_momenta(sine_table, source[1])
    imag_part = along_momenta(cosine_table, source[1]) - along_momenta(sine_table, source[0])
    return jnp.stack([real_part, imag_part]) * factor


def self_energy(less_tiles, great_tiles, screen_tiles, cosine_table, sine_table):
    lesser = to_real(less_tiles, cosine_table, sine_table)
    greater = to_real(great_tiles, cosine_table, sine_table)
    screen_real = to_real(screen_tiles, cosine_table, sine_table)
    polar_real = lesser[0] * greater[1] - lesser[1] * greater[0]
    polar_imag = lesser[0] * greater[0] + lesser[1] * greater[1]
    inter_real = screen_real[0] + polar_real
    inter_imag = screen_real[1] + polar_imag
    sigma_re = -(lesser[0] * inter_imag + lesser[1] * inter_real)
    sigma_im = lesser[0] * inter_real - lesser[1] * inter_imag
    return to_momentum(jnp.stack([sigma_re, sigma_im]), cosine_table, sine_table)


def batch_product(left, right):
    return jnp.einsum(
        "kis,ksj->kij",
        left,
        right,
        precision=lax.Precision.HIGHEST,
        preferred_element_type=jnp.float32,
    )


def complex_product(left, right):
    real_part = batch_product(left[0], right[0]) - batch_product(left[1], right[1])
    imag_part = batch_product(left[0], right[1]) + batch_product(left[1], right[0])
    return jnp.stack([real_part, imag_part])


def body(green_less, green_great, screened):
    momenta = green_less.shape[1] * lax.axis_size("ka")
    cosine_table, sine_table = angle_tables(momenta)
    sigma_tiles = lax.all_to_all(
        self_energy(
            lax.all_to_all(green_less, "ka", split_axis=2, concat_axis=1, tiled=True),
            lax.all_to_all(green_great, "ka", split_axis=2, concat_axis=1, tiled=True),
            lax.all_to_all(screened, "ka", split_axis=2, concat_axis=1, tiled=True),
            cosine_table,
            sine_table,
        ),
        "ka",
        split_axis=1,
        concat_axis=2,
        tiled=True,
    )
    column_panel = lax.all_gather(green_less, "tr", axis=2, tiled=True)
    summed = complex_product(lax.all_gather(sigma_tiles, "tc", axis=3, tiled=True), column_panel)
    collision = summed * NT ** (-0.5)
    return (collision, green_less + collision)


def solution(mesh):
    in_specs = (P(None, "ka", "tr", "tc"), P(None, "ka", "tr", "tc"), P(None, "ka", "tr", "tc"))
    out_specs = (P(None, "ka", "tr", "tc"), P(None, "ka", "tr", "tc"))
    return jax.shard_map(body, mesh=mesh, in_specs=in_specs, out_specs=out_specs, check_vma=False)
```

profile of v0, /device:TPU:1, one launch (start us, length us, event | category | flops | bytes accessed | tf_op | source)
XLA Modules:
  0.0 266.4 jit_solution(5793646412172666438)
XLA Ops:
  7.2 0.0 copy-start.1
  7.2 3.1 %copy.48 = f32[2,1,512,256]{3,0,1,2:T(2,128)} copy(f32[2,1,512,256]{3,2,1,0:T(8,128)} %param.5) | data formatting | bytes 2097152 | tf_op args[2]
  10.3 10.0 %all-to-all-start.1 = ((f32[2,1,512,256]{3,0,1,2:T(2,128)}), f32[2,1,512,256]{3,0,1,2:T(2,128)S(1)}, u32[]{:S(2)}, u32[]{:S(2)}) async-start(f32[2,1,512,256]{3,0,1,2:T(2,128)} %copy.48), calls=%async_computation.1 | async-start | bytes 2097152 | tf_op jit(solution)/shard_map/all_to_all | solution.py:72
  20.3 1.8 copy.41
  22.1 26.0 %all-to-all-done.1 = f32[2,1,512,256]{3,0,1,2:T(2,128)S(1)} async-done(((f32[2,1,512,256]{3,0,1,2:T(2,128)}), f32[2,1,512,256]{3,0,1,2:T(2,128)S(1)}, u32[]{:S(2)}, u32[]{:S(2)}) %all-to-all-start.1) | async-done | bytes 1048608 | tf_op jit(solution)/shard_map/all_to_all | solution.py:72
  48.1 3.9 %all-to-all-start = ((f32[2,1,512,256]{3,0,1,2:T(2,128)}), f32[2,1,512,256]{3,0,1,2:T(2,128)S(1)}, u32[]{:S(2)}, u32[]{:S(2)}) async-start(f32[2,1,512,256]{3,0,1,2:T(2,128)} %copy.41), calls=%async_computation | async-start | bytes 2097152 | tf_op jit(solution)/shard_map/all_to_all | solution.py:70
  52.0 0.0 all-gather.5.cloned.1.call-start
  52.0 0.7 all-gather.5.cloned.1.call-update
  52.7 1.8 copy.55
  54.5 70.3 %all-to-all-done = f32[2,1,512,256]{3,0,1,2:T(2,128)S(1)} async-done(((f32[2,1,512,256]{3,0,1,2:T(2,128)}), f32[2,1,512,256]{3,0,1,2:T(2,128)S(1)}, u32[]{:S(2)}, u32[]{:S(2)}) %all-to-all-start) | async-done | bytes 1048608 | tf_op jit(solution)/shard_map/all_to_all | solution.py:70
  124.8 3.9 %all-to-all-start.2 = ((f32[2,1,512,256]{3,0,1,2:T(2,128)}), f32[2,1,512,256]{3,0,1,2:T(2,128)S(1)}, u32[]{:S(2)}, u32[]{:S(2)}) async-start(f32[2,1,512,256]{3,0,1,2:T(2,128)} %copy.55), calls=%async_computation.2 | async-start | bytes 2097152 | tf_op jit(solution)/shard_map/all_to_all | solution.py:71
  128.7 0.2 all-gather.3.cloned.1.call-start
  128.9 0.8 fusion.145
  129.8 0.8 fusion.143
  130.7 0.9 fusion.24
  131.6 0.9 fusion.12
  132.6 0.9 fusion.28
  133.5 0.9 fusion.13
  134.4 0.9 fusion.34
  135.3 0.9 fusion.15
  136.2 0.9 fusion.30
  137.1 0.9 fusion.14
  138.0 18.6 %all-to-all-done.2 = f32[2,1,512,256]{3,0,1,2:T(2,128)S(1)} async-done(((f32[2,1,512,256]{3,0,1,2:T(2,128)}), f32[2,1,512,256]{3,0,1,2:T(2,128)S(1)}, u32[]{:S(2)}, u32[]{:S(2)}) %all-to-all-start.2) | async-done | bytes 1048608 | tf_op jit(solution)/shard_map/all_to_all | solution.py:71
  156.6 0.8 fusion.144
  157.5 0.9 fusion.18
  158.4 0.9 fusion.22
  159.3 1.1 fusion.10
  160.4 0.9 fusion.11
  161.3 0.1 maximum_multiply_fusion.2
  161.4 0.2 maximum_multiply_fusion
  161.7 0.4 add_negate_fusion
  162.1 0.7 fusion.49
  162.7 0.7 fusion.47
  163.4 0.7 fusion.9
  164.1 0.7 fusion.8
  164.7 0.1 maximum_multiply_fusion.3
  164.9 0.6 copy.62
  165.5 31.5 %all_to_all.19 = f32[2,32,16,256]{3,2,0,1:T(8,128)S(1)} all-to-all(f32[2,32,16,256]{3,2,0,1:T(8,128)S(1)} %copy.62), channel_id=1, replica_groups=mesh['ka'=32,'tr'=2,'tc'=4] {'ka'}, dimensions={1} | all-to-all | bytes 2097152 | tf_op jit(solution)/shard_map/all_to_all | solution.py:68
  197.0 1.1 copy.63
  198.0 0.0 all-gather.3.cloned.1.call-update
  198.1 0.0 all-gather.5.cloned.1.call-done
  198.1 49.0 %all-gather.3.cloned.1.call-done = f32[2,1,512,1024]{3,2,0,1:T(8,128)} async-done(((f32[2,1,512,256]{3,2,0,1:T(8,128)}), f32[2,1,512,1024]{3,2,0,1:T(8,128)}) %all-gather.3.cloned.1.call-update) | async-done | bytes 4194320 | tf_op jit(solution)/shard_map/all_gather | solution.py:82
  247.2 3.8 %fusion.1 = f32[512,256]{1,0:T(8,128)S(1)} fusion(f32[2,1,512,1024]{3,2,0,1:T(8,128)} %all-gather.3.cloned.1.call-done, f32[2,1,1024,256]{3,2,1,0:T(8,128)} %all-gather.5.cloned.1.call-done), kind=kOutput, calls=%fused_computation.3 | convolution fusion | flops 1610612736 | bytes 3670016 | tf_op jit(solution)/shard_map/kis,ksj->kij/dot_general | solution.py:50
  251.0 3.4 %fusion = f32[512,256]{1,0:T(8,128)S(1)} fusion(f32[2,1,512,1024]{3,2,0,1:T(8,128)} %all-gather.3.cloned.1.call-done, f32[2,1,1024,256]{3,2,1,0:T(8,128)S(1)} %copy-done.3), kind=kOutput, calls=%fused_computation.2 | convolution fusion | flops 1610612736 | bytes 3670016 | tf_op jit(solution)/shard_map/kis,ksj->kij/dot_general | solution.py:50
  254.4 1.8 fusion.5
  256.2 0.0 copy-start.2
  256.2 1.8 fusion.7
  258.1 1.5 fusion.142
  (14 shorter events, 0.2 us)
Async XLA Ops:
  7.2 13.1 %copy-start.1 = (f32[2,1,512,256]{3,2,1,0:T(8,128)S(1)}, f32[2,1,512,256]{3,2,1,0:T(8,128)}, u32[]{:S(2)}) copy-start(f32[2,1,512,256]{3,2,1,0:T(8,128)} %param.3) | copy-start | bytes 3145732
  10.3 37.9 %all-to-all-start.1 = ((f32[2,1,512,256]{3,0,1,2:T(2,128)}), f32[2,1,512,256]{3,0,1,2:T(2,128)S(1)}, u32[]{:S(2)}, u32[]{:S(2)}) async-start(f32[2,1,512,256]{3,0,1,2:T(2,128)} %copy.48), calls=%async_computation.1 | async-start | bytes 2097152 | tf_op jit(solution)/shard_map/all_to_all | solution.py:72
  22.1 30.7 %copy-start.4 = (f32[2,1,512,256]{3,2,1,0:T(8,128)S(1)}, f32[2,1,512,256]{3,2,1,0:T(8,128)}, u32[]{:S(2)}) copy-start(f32[2,1,512,256]{3,2,1,0:T(8,128)} %param.4) | copy-start | bytes 3145732
  48.1 76.7 %all-to-all-start = ((f32[2,1,512,256]{3,0,1,2:T(2,128)}), f32[2,1,512,256]{3,0,1,2:T(2,128)S(1)}, u32[]{:S(2)}, u32[]{:S(2)}) async-start(f32[2,1,512,256]{3,0,1,2:T(2,128)} %copy.41), calls=%async_computation | async-start | bytes 2097152 | tf_op jit(solution)/shard_map/all_to_all | solution.py:70
  52.0 146.1 %all-gather.5.cloned.1.call-start = ((), (), s32[]{:S(2)}) async-start(), calls=%async_computation.5 | async-start | bytes 3145728 | tf_op jit(solution)/shard_map/all_gather | solution.py:81
  124.8 31.8 %all-to-all-start.2 = ((f32[2,1,512,256]{3,0,1,2:T(2,128)}), f32[2,1,512,256]{3,0,1,2:T(2,128)S(1)}, u32[]{:S(2)}, u32[]{:S(2)}) async-start(f32[2,1,512,256]{3,0,1,2:T(2,128)} %copy.55), calls=%async_computation.2 | async-start | bytes 2097152 | tf_op jit(solution)/shard_map/all_to_all | solution.py:71
  128.7 118.4 %all-gather.3.cloned.1.call-start = ((), (), s32[]{:S(2)}) async-start(), calls=%async_computation.4 | async-start | bytes 5242880 | tf_op jit(solution)/shard_map/all_gather | solution.py:82
  198.1 52.9 %copy-start.3 = (f32[2,1,1024,256]{3,2,1,0:T(8,128)S(1)}, f32[2,1,1024,256]{3,2,1,0:T(8,128)}, u32[]{:S(2)}) copy-start(f32[2,1,1024,256]{3,2,1,0:T(8,128)} %all-gather.5.cloned.1.call-done) | copy-start | bytes 6291460
  247.1 7.2 %copy-start = (f32[2,1,512,1024]{3,2,0,1:T(8,128)S(1)}, f32[2,1,512,1024]{3,2,0,1:T(8,128)}, u32[]{:S(2)}) copy-start(f32[2,1,512,1024]{3,2,0,1:T(8,128)} %all-gather.3.cloned.1.call-done) | copy-start | bytes 12582916
  256.2 1.8 copy-start.2
Sparse Core Ops, SparseCore 0:
  54.6 55.5 all-gather.4
  198.2 48.9 all-gather.2
where the time goes:
time: 267 us; the launch traced here: 266 us
  waiting for transfers between devices  165 us (62%)
  blocking collectives  31.5 us (12%)
  matrix products  24.4 us (9%)
  starting transfers between devices  18 us (7%)
  between operations  14.4 us (5%)
  local copies, waits for them, and re-layouts  11 us (4%)
    all_to_all x1, waiting for transfers between devices, body(): lax.all_to_all(green_less, 'ka', split_axis=2, concat_axis=1, tiled=True)  70.3 us
    all_gather x1, waiting for transfers between devices, body(): lax.all_gather(sigma_tiles, 'tc', axis=3, tiled=True)  49 us
    all_to_all x1, blocking collectives, body(): lax.all_to_all(self_energy(lax.all_to_all(green_less, 'ka', split_axis=2,...  31.5 us
    all_to_all x1, waiting for transfers between devices, body(): lax.all_to_all(screened, 'ka', split_axis=2, concat_axis=1, tiled=True)  26 us
    all_to_all x1, waiting for transfers between devices, body(): lax.all_to_all(green_great, 'ka', split_axis=2, concat_axis=1, tiled=True)  18.6 us
    dot_general x16, matrix products, along_momenta(): jnp.tensordot(matrix_in, source, axes=1, precision=lax.Precision.HIGHEST)  13.6 us
    dot_general x4, matrix products, batch_product(): jnp.einsum('kis,ksj->kij', left, right, precision=lax.Precision.HIGHEST,...  10.8 us
    all_to_all x1, starting transfers between devices, body(): lax.all_to_all(screened, 'ka', split_axis=2, concat_axis=1, tiled=True)  10 us
  transfers between devices with their start and end apart: 5, of which 4 were waited for; matrix products, arithmetic and copies ran while one was open for 8% of the time, Pallas kernels for 0%

commit v1 on v0

v1 whole, which is shorter than its diff:
```python
import functools
import math

import jax
import jax.numpy as jnp
from jax import lax
from jax.experimental import pallas as pl
from jax.experimental.pallas import tpu as pltpu
from jax.sharding import PartitionSpec as P

MESH = pl.DeviceIdType.MESH
CHUNKS = 2
ROWS = 512
COLS = 256
CROWS = ROWS // CHUNKS
ZROWS = CROWS // 4
TROWS = ZROWS // 8
INNER = 32.0 ** -0.5
OUTER = 1.0 / (32.0 * math.sqrt(32.0) * 32.0)


def cmul(value, turns):
    turns = turns % 32
    re, im = value
    if turns == 0:
        return value
    if turns == 8:
        return -im, re
    if turns == 16:
        return -re, -im
    if turns == 24:
        return im, -re
    cos, sin = math.cos(2 * math.pi * turns / 32), math.sin(2 * math.pi * turns / 32)
    if turns % 8 == 4:
        root = math.sqrt(0.5)
        plus, minus = (re + im) * root, (re - im) * root
        return {4: (minus, plus), 12: (-plus, minus), 20: (-minus, -plus), 28: (plus, -minus)}[turns]
    return re * cos - im * sin, re * sin + im * cos


def cadd(a, b):
    return a[0] + b[0], a[1] + b[1]


def csub(a, b):
    return a[0] - b[0], a[1] - b[1]


def dft(values, sign):
    size = len(values)
    if size == 1:
        return values
    even, odd = dft(values[0::2], sign), dft(values[1::2], sign)
    step = 32 // size
    low, high = [], []
    for m in range(size // 2):
        turned = cmul(odd[m], sign * step * m)
        low.append(cadd(even[m], turned))
        high.append(csub(even[m], turned))
    return low + high


def split(value):
    high = value.astype(jnp.bfloat16)
    return high, (value - high.astype(jnp.float32)).astype(jnp.bfloat16)


def kernel(
    less, great, screen, collision, green_next,
    zbuf, tile, mid, mid2, sig, back, sigma, gloc, grem, ghigh, glow, acc,
    own_sem, zs, zr, xs, xr, ts, tr_, bs, br, cs, cr, ys, yr, fs, fr,
):
    ka, h, y = lax.axis_index("ka"), lax.axis_index("tr"), lax.axis_index("tc")
    x, z, c = ka // 8, (ka // 2) % 4, ka % 2
    xc = x * 2 + c

    def at(xx, zz, cc):
        return xx * 8 + zz * 2 + cc

    zpeers = [3 - z, (z + 2) % 4, z + 1 - 2 * (z % 2)]
    xpeers = [((x + 1) % 4, c), ((x + 3) % 4, 1 - c), ((x + 1) % 4, 1 - c), ((x + 3) % 4, c), ((x + 2) % 4, c), ((x + 2) % 4, 1 - c), (x, 1 - c)]
    up, down = (y + 1) % 4, (y + 3) % 4

    barrier = pltpu.get_barrier_semaphore()
    peers = [(at(x, zz, c), h, y) for zz in zpeers]
    peers += [(at(x, zz, c), 1 - h, y) for zz in range(4)]
    peers += [(at(xx, z, cc), h, y) for xx, cc in xpeers]
    peers += [(ka, h, up), (ka, h, down)]
    for peer in peers:
        pl.semaphore_signal(barrier, inc=1, device_id=peer, device_id_type=MESH)
    pl.semaphore_wait(barrier, len(peers))

    arrays = (less, great, screen)
    pending = []

    def remote(src, dst, send, recv, peer):
        copy = pltpu.make_async_remote_copy(
            src_ref=src, dst_ref=dst, send_sem=send, recv_sem=recv, device_id=peer, device_id_type=MESH
        )
        copy.start()
        pending.append(copy)

    def arrived(ref, sem, send):
        pltpu.make_async_remote_copy(
            src_ref=ref, dst_ref=ref, send_sem=send, recv_sem=sem, device_id=(ka, h, y), device_id_type=MESH
        ).wait_recv()

    def rows(start, size):
        return pl.ds(pl.multiple_of(start, 8), size)

    load = pltpu.make_async_copy(less.at[:, 0], gloc, own_sem.at[0])
    for n in range(CHUNKS):
        for a in range(3):
            for i, zz in enumerate(zpeers):
                remote(
                    arrays[a].at[:, 0, rows(n * CROWS + zz * ZROWS, ZROWS), :],
                    zbuf.at[n, a, z], zs.at[n, a, i], zr.at[n, a, i], (at(x, zz, c), h, y),
                )
    own = [
        [
            pltpu.make_async_copy(
                arrays[a].at[:, 0, rows(n * CROWS + z * ZROWS, ZROWS), :], zbuf.at[n, a, z], own_sem.at[1 + 3 * n + a]
            )
            for a in range(3)
        ]
        for n in range(CHUNKS)
    ]
    for n in range(CHUNKS):
        for a in range(3):
            own[n][a].start()
    load.start()

    def forward_x(n, a):
        own[n][a].wait()
        for i, zz in enumerate(zpeers):
            arrived(zbuf.at[n, a, zz], zr.at[n, a, i], zs.at[n, a, i])
        for i, (xx, cc) in enumerate(xpeers):
            remote(
                zbuf.at[n, a, :, :, rows((xx * 2 + cc) * TROWS, TROWS), :],
                tile.at[n, a, xc], xs.at[n, a, i], xr.at[n, a, i], (at(xx, z, cc), h, y),
            )
        tile[n, a, xc] = zbuf[n, a, :, :, rows(xc * TROWS, TROWS), :]

    mirror = [3, 2, 1, 0, 4, 5, 6]
    mirror = [3, 2, 1, 0, 4, 5, 6]

    def transform(n):
        for a in range(3):
            for i in range(7):
                sender_xx, sender_cc = xpeers[mirror_of[i]]
                arrived(tile.at[n, a, sender_xx * 2 + sender_cc], xr.at[n, a, i], xs.at[n, a, i])

        def column(q, carry):
            cols = pl.ds(pl.multiple_of(q * 128, 128), 128)

            for a in range(3):
                for k2 in range(8):
                    j, cc = k2 // 2, k2 % 2
                    values = [
                        (tile[n, a, 2 * xx + cc, j, 0, :, cols], tile[n, a, 2 * xx + cc, j, 1, :, cols])
                        for xx in range(4)
                    ]
                    for r1, value in enumerate(dft(values, 1)):
                        re, im = cmul(value, k2 * r1)
                        mid[a, r1, k2, 0], mid[a, r1, k2, 1] = re, im
            for r1 in range(4):
                sides = [dft([(mid[a, r1, k2, 0], mid[a, r1, k2, 1]) for k2 in range(8)], 1) for a in range(3)]
                out = []
                for (lr, li), (gr, gi), (wr, wi) in zip(*sides):
                    ir = OUTER * wr + (OUTER * INNER) * (lr * gi - li * gr)
                    ii = OUTER * wi + (OUTER * INNER) * (lr * gr + li * gi)
                    out.append((-(lr * ii + li * ir), lr * ir - li * ii))
                for k2, value in enumerate(dft(out, -1)):
                    re, im = cmul(value, -k2 * r1)
                    mid2[r1, k2, 0], mid2[r1, k2, 1] = re, im
            for k2 in range(8):
                j, cc = k2 // 2, k2 % 2
                for xx, (re, im) in enumerate(dft([(mid2[r1, k2, 0], mid2[r1, k2, 1]) for r1 in range(4)], -1)):
                    sig[n, 2 * xx + cc, j, 0, :, cols] = re
                    sig[n, 2 * xx + cc, j, 1, :, cols] = im
            return carry

        lax.fori_loop(0, COLS // 128, column, 0)
        for i, (xx, cc) in enumerate(xpeers):
            remote(
                sig.at[n, xx * 2 + cc], back.at[n, :, :, rows(xc * TROWS, TROWS), :],
                bs.at[n, i], br.at[n, i], (at(xx, z, cc), h, y),
            )
        back[n, :, :, rows(xc * TROWS, TROWS), :] = sig[n, xc]

    mirror_of = mirror

    def back_z(n):
        for i in range(7):
            sender_xx, sender_cc = xpeers[mirror_of[i]]
            arrived(back.at[n, :, :, rows((sender_xx * 2 + sender_cc) * TROWS, TROWS), :], br.at[n, i], bs.at[n, i])
        for i, zz in enumerate(zpeers):
            remote(
                back.at[n, zz], sigma.at[y, :, rows(n * CROWS + z * ZROWS, ZROWS), :],
                cs.at[n, i], cr.at[n, i], (at(x, zz, c), h, y),
            )
        sigma[y, :, rows(n * CROWS + z * ZROWS, ZROWS), :] = back[n, z]

    def share_less(n):
        for i, zz in enumerate([z] + zpeers):
            remote(
                zbuf.at[n, 0, zz], grem.at[:, rows(n * CROWS + z * ZROWS, ZROWS), :],
                ts.at[n, i], tr_.at[n, i], (at(x, zz, c), 1 - h, y),
            )

    def wait_less(n):
        for i, zz in enumerate([z] + zpeers):
            arrived(grem.at[:, rows(n * CROWS + zz * ZROWS, ZROWS), :], tr_.at[n, i], ts.at[n, i])

    def spread_y(n):
        for i, zz in enumerate(zpeers):
            arrived(sigma.at[y, :, rows(n * CROWS + zz * ZROWS, ZROWS), :], cr.at[n, i], cs.at[n, i])
        block = sigma.at[y, :, pl.ds(n * CROWS, CROWS), :]
        remote(block, block, ys.at[n, 0], yr.at[n, 0], (ka, h, up))
        remote(block, block, ys.at[n, 1], yr.at[n, 1], (ka, h, down))

    def relay_y(n):
        half = CROWS // 2
        arrived(sigma.at[down, :, pl.ds(n * CROWS, CROWS), :], yr.at[n, 0], ys.at[n, 0])
        block = sigma.at[down, :, pl.ds(n * CROWS, half), :]
        remote(block, block, fs.at[n, 0], fr.at[n, 0], (ka, h, up))
        arrived(sigma.at[up, :, pl.ds(n * CROWS, CROWS), :], yr.at[n, 1], ys.at[n, 1])
        block = sigma.at[up, :, pl.ds(n * CROWS + half, half), :]
        remote(block, block, fs.at[n, 1], fr.at[n, 1], (ka, h, down))

    def wait_y(n):
        half = CROWS // 2
        far = (y + 2) % 4
        arrived(sigma.at[far, :, pl.ds(n * CROWS, half), :], fr.at[n, 0], fs.at[n, 0])
        arrived(sigma.at[far, :, pl.ds(n * CROWS + half, half), :], fr.at[n, 1], fs.at[n, 1])

    def prepare(source, part):
        for s in range(2):
            re, im = source[0, s * 256:(s + 1) * 256, :], source[1, s * 256:(s + 1) * 256, :]
            for value, places in ((re, ((0, 0), (1, 256))), (im, ((0, 256),)), (-im, ((1, 0),))):
                high, low = split(value)
                for ri, col in places:
                    ghigh[part * 2 + s, ri, :, col:col + 256] = high
                    glow[part * 2 + s, ri, :, col:col + 256] = low

    def multiply(n, part, first):
        def block(s, carry):
            index = part * 2 + s
            total = None
            for ri in range(2):
                high, low = split(sigma[index, ri, pl.ds(n * CROWS, CROWS), :])
                for left, right in ((high, ghigh), (high, glow), (low, ghigh)):
                    product = jnp.dot(left, right[index, ri], preferred_element_type=jnp.float32)
                    total = product if total is None else total + product
            acc[n] += total
            return carry

        if first:
            acc[n] = jnp.zeros_like(acc[n])
        lax.fori_loop(0, 2, block, 0)

    def finish(n):
        span = pl.ds(n * CROWS, CROWS)
        for ri in range(2):
            value = acc[n, :, ri * 256:(ri + 1) * 256]
            collision[ri, 0, span, :] = value
            green_next[ri, 0, span, :] = gloc[ri, span, :] + value

    load.wait()
    prepare(gloc, h)
    forward_x(0, 0)
    forward_x(0, 1)
    forward_x(0, 2)
    transform(0)
    forward_x(1, 0)
    back_z(0)
    share_less(0)
    forward_x(1, 1)
    forward_x(1, 2)
    transform(1)
    back_z(1)
    share_less(1)
    spread_y(0)
    relay_y(0)
    spread_y(1)
    wait_y(0)
    multiply(0, h, True)
    relay_y(1)
    wait_less(0)
    wait_less(1)
    prepare(grem, 1 - h)
    multiply(0, 1 - h, False)
    finish(0)
    wait_y(1)
    multiply(1, h, True)
    multiply(1, 1 - h, False)
    finish(1)
    for copy in pending:
        copy.wait_send()


def body(green_less, green_great, screened):
    dma = pltpu.SemaphoreType.DMA
    block = jax.ShapeDtypeStruct(green_less.shape, jnp.float32)
    f32, bf16 = jnp.float32, jnp.bfloat16
    return pl.pallas_call(
        kernel,
        out_shape=(block, block),
        in_specs=[pl.BlockSpec(memory_space=pl.ANY)] * 3,
        out_specs=(pl.BlockSpec(memory_space=pltpu.VMEM),) * 2,
        scratch_shapes=[
            pltpu.VMEM((CHUNKS, 3, 4, 2, ZROWS, COLS), f32),
            pltpu.VMEM((CHUNKS, 3, 8, 4, 2, TROWS, COLS), f32),
            pltpu.VMEM((3, 4, 8, 2, TROWS, 128), f32),
            pltpu.VMEM((4, 8, 2, TROWS, 128), f32),
            pltpu.VMEM((CHUNKS, 8, 4, 2, TROWS, COLS), f32),
            pltpu.VMEM((CHUNKS, 4, 2, ZROWS, COLS), f32),
            pltpu.VMEM((4, 2, ROWS, COLS), f32),
            pltpu.VMEM((2, ROWS, COLS), f32),
            pltpu.VMEM((2, ROWS, COLS), f32),
            pltpu.VMEM((4, 2, 256, 512), bf16),
            pltpu.VMEM((4, 2, 256, 512), bf16),
            pltpu.VMEM((CHUNKS, CROWS, 512), f32),
            dma((1 + 3 * CHUNKS,)),
            dma((CHUNKS, 3, 3)), dma((CHUNKS, 3, 3)),
            dma((CHUNKS, 3, 7)), dma((CHUNKS, 3, 7)),
            dma((CHUNKS, 4)), dma((CHUNKS, 4)),
            dma((CHUNKS, 7)), dma((CHUNKS, 7)),
            dma((CHUNKS, 3)), dma((CHUNKS, 3)),
            dma((CHUNKS, 2)), dma((CHUNKS, 2)),
            dma((CHUNKS, 2)), dma((CHUNKS, 2)),
        ],
        compiler_params=pltpu.CompilerParams(collective_id=0, has_side_effects=True, vmem_limit_bytes=56 << 20),
        name="collide",
    )(green_less, green_great, screened)


def solution(mesh):
    spec = P(None, "ka", "tr", "tc")
    return jax.shard_map(body, mesh=mesh, in_specs=(spec,) * 3, out_specs=(spec,) * 2, check_vma=False)
```

time: 267 us -> 153 us (0.57)
  waiting for transfers between devices: 165 us -> 0 us
  Pallas kernels: 0 us -> 149 us
  blocking collectives: 31.5 us -> 0 us
  matrix products: 24.4 us -> 0 us
  starting transfers between devices: 18 us -> 0 us
  between operations: 14.4 us -> 0.65 us
  local copies, waits for them, and re-layouts: 11 us -> 3.32 us
    pallas_call x0 -> x1, Pallas kernels: none -> 149 us  [body(): pl.pallas_call(kernel, out_shape=(block, block), in_specs=[pl.BlockSpec(m...]
    all_to_all x3 -> x0, waiting for transfers between devices: 115 us -> none  [the longest x1 70.3 us: body(): lax.all_to_all(green_less, 'ka', split_axis=2, concat_axis=1, tiled=True)]
    all_gather x2 -> x0, waiting for transfers between devices: 49.1 us -> none  [the longest x1 49 us: body(): lax.all_gather(sigma_tiles, 'tc', axis=3, tiled=True)]
    all_to_all x1 -> x0, blocking collectives: 31.5 us -> none  [body(): lax.all_to_all(self_energy(lax.all_to_all(green_less, 'ka', split_axis=2,...]
    dot_general x20 -> x0, matrix products: 24.4 us -> none  [the longest x16 13.6 us: along_momenta(): jnp.tensordot(matrix_in, source, axes=1, precision=lax.Precision.HIGHEST)]
    all_to_all x3 -> x0, starting transfers between devices: 17.7 us -> none  [the longest x1 10 us: body(): lax.all_to_all(screened, 'ka', split_axis=2, concat_axis=1, tiled=True)]
    unnamed x19 -> x4, local copies, waits for them, and re-layouts: 6.89 us -> 3.32 us
  transfers between devices with their start and end apart: 5 -> 0, of which waited for: 4 -> 0; matrix products, arithmetic and copies ran while one was open for 8% -> 0% of each run, Pallas kernels for 0% -> 0%
where the time goes in v1:
time: 153 us
  Pallas kernels  149 us (97%)
  local copies, waits for them, and re-layouts  3.32 us (2%)
    pallas_call x1, Pallas kernels, body(): pl.pallas_call(kernel, out_shape=(block, block), in_specs=[pl.BlockSpec(m...  149 us
    unnamed x4, local copies, waits for them, and re-layouts  3.32 us

profile of v1, /device:TPU:1, one launch (start us, length us, event | category | flops | bytes accessed | tf_op | source)
XLA Modules:
  0.0 152.9 jit_solution(1674628678294317934)
XLA Ops:
  0.6 148.9 %collide.1 = (f32[2,1,512,256]{3,2,1,0:T(8,128)}, f32[2,1,512,256]{3,2,1,0:T(8,128)}) custom-call(f32[2,1,512,256]{3,2,1,0:T(8,128)} %less.1, f32[2,1,512,256]{3,2,1,0:T(8,128)} %great.1, f32[2,1,512,256]{3,2,1,0:T(8,128)} %screen.1), custom_call_target="tpu_custom_call" | custom-call | tf_op jit(solution)/shard_map/collide/pallas_call | solution.py:306
  149.6 0.0 copy-start
  149.6 2.4 %copy.7 = f32[2,1,512,256]{3,2,1,0:T(8,128)} copy(f32[2,1,512,256]{3,2,1,0:T(8,128)} %get-tuple-element.4) | data formatting | bytes 2097152
  151.9 0.0 copy-done
  151.9 1.0 copy.8
Async XLA Ops:
  149.6 2.4 %copy-start = (f32[2,1,512,256]{3,2,1,0:T(8,128)S(1)}, f32[2,1,512,256]{3,2,1,0:T(8,128)}, u32[]{:S(2)}) copy-start(f32[2,1,512,256]{3,2,1,0:T(8,128)} %get-tuple-element.5) | copy-start | bytes 3145732

commit v2 on v1

v2 whole, which is shorter than its diff:
```python
import functools
import math

import jax
import jax.numpy as jnp
from jax import lax
from jax.experimental import pallas as pl
from jax.experimental.pallas import tpu as pltpu
from jax.sharding import PartitionSpec as P

MESH = pl.DeviceIdType.MESH
ROWS = 512
COLS = 256
CHUNKS = 4
CROWS = 256
CCOLS = 128
ZROWS = CROWS // 4
TROWS = ZROWS // 8
INNER = 32.0 ** -0.5
OUTER = 1.0 / (32.0 * math.sqrt(32.0))
NORM = 1.0 / 32.0


def cmul(value, turns):
    turns = turns % 32
    re, im = value
    if turns == 0:
        return value
    if turns == 8:
        return -im, re
    if turns == 16:
        return -re, -im
    if turns == 24:
        return im, -re
    cos, sin = math.cos(2 * math.pi * turns / 32), math.sin(2 * math.pi * turns / 32)
    if turns % 8 == 4:
        root = math.sqrt(0.5)
        plus, minus = (re + im) * root, (re - im) * root
        return {4: (minus, plus), 12: (-plus, minus), 20: (-minus, -plus), 28: (plus, -minus)}[turns]
    return re * cos - im * sin, re * sin + im * cos


def cadd(a, b):
    return a[0] + b[0], a[1] + b[1]


def csub(a, b):
    return a[0] - b[0], a[1] - b[1]


def dft(values, sign):
    size = len(values)
    if size == 1:
        return values
    even, odd = dft(values[0::2], sign), dft(values[1::2], sign)
    step = 32 // size
    low, high = [], []
    for m in range(size // 2):
        turned = cmul(odd[m], sign * step * m)
        low.append(cadd(even[m], turned))
        high.append(csub(even[m], turned))
    return low + high


def split(value):
    high = value.astype(jnp.bfloat16)
    return high, (value - high.astype(jnp.float32)).astype(jnp.bfloat16)


def kernel(
    less, great, screen, product,
    zbuf, tile, mid, mid2, sig, back, sigma, gloc, grem, ghigh, glow, acc,
    own_sem, out_sem, zs, zr, xs, xr, ts, tr, bs, br, cs, cr, ys, yr, fs, fr,
):
    ka, h, y = lax.axis_index("ka"), lax.axis_index("tr"), lax.axis_index("tc")
    x, z, c = ka // 8, (ka // 2) % 4, ka % 2
    xc = x * 2 + c
    arrays = (less, great, screen)
    pending = []

    def at(xx, zz, cc):
        return xx * 8 + zz * 2 + cc

    zpeers = [3 - z, (z + 2) % 4, z + 1 - 2 * (z % 2)]
    xpeers = [
        ((x + 1) % 4, c), ((x + 3) % 4, 1 - c), ((x + 1) % 4, 1 - c), ((x + 3) % 4, c),
        ((x + 2) % 4, c), ((x + 2) % 4, 1 - c), (x, 1 - c),
    ]
    opposite = [3, 2, 1, 0, 4, 5, 6]
    up, down = (y + 1) % 4, (y + 3) % 4

    def remote(src, dst, send, recv, peer):
        copy = pltpu.make_async_remote_copy(
            src_ref=src, dst_ref=dst, send_sem=send, recv_sem=recv, device_id=peer, device_id_type=MESH
        )
        copy.start()
        pending.append(copy)

    def arrived(ref, sem, send):
        pltpu.make_async_remote_copy(
            src_ref=ref, dst_ref=ref, send_sem=send, recv_sem=sem, device_id=(ka, h, y), device_id_type=MESH
        ).wait_recv()

    def rows(start, size):
        return pl.ds(pl.multiple_of(start, 8), size)

    def zrows(m, zz):
        return rows((m // 2) * CROWS + zz * ZROWS, ZROWS)

    def cols(m):
        return pl.ds((m % 2) * CCOLS, CCOLS)

    def xrows(index):
        return rows(index * TROWS, TROWS)

    own = [
        [
            pltpu.make_async_copy(arrays[a].at[:, 0, zrows(m, z), cols(m)], zbuf.at[m, a, z], own_sem.at[1 + 3 * m + a])
            for a in range(3)
        ]
        for m in range(CHUNKS)
    ]
    load = pltpu.make_async_copy(less.at[:, 0], gloc, own_sem.at[0])

    def send_z(m, a):
        for i, zz in enumerate(zpeers):
            remote(
                arrays[a].at[:, 0, zrows(m, zz), cols(m)], zbuf.at[m, a, z],
                zs.at[m, a, i], zr.at[m, a, i], (at(x, zz, c), h, y),
            )

    def send_x(m, a):
        own[m][a].wait()
        for i, zz in enumerate(zpeers):
            arrived(zbuf.at[m, a, zz], zr.at[m, a, i], zs.at[m, a, i])
        for i, (xx, cc) in enumerate(xpeers):
            remote(
                zbuf.at[m, a, :, :, xrows(xx * 2 + cc), :], tile.at[m, a, xc],
                xs.at[m, a, i], xr.at[m, a, i], (at(xx, z, cc), h, y),
            )
        tile[m, a, xc] = zbuf[m, a, :, :, xrows(xc), :]

    def arrive_z(m, a):
        own[m][a].wait()
        for i, zz in enumerate(zpeers):
            arrived(zbuf.at[m, a, zz], zr.at[m, a, i], zs.at[m, a, i])

    def arrive_x(m, a):
        for i in range(7):
            xx, cc = xpeers[opposite[i]]
            arrived(tile.at[m, a, xx * 2 + cc], xr.at[m, a, i], xs.at[m, a, i])

    def arrive_c(m):
        for i, zz in enumerate(zpeers):
            arrived(sigma.at[y, m % 2, :, zrows(m, zz), :], cr.at[m, i], cs.at[m, i])

    def share_less(m):
        for i, zz in enumerate([z] + zpeers):
            remote(
                zbuf.at[m, 0, zz], grem.at[:, zrows(m, z), cols(m)],
                ts.at[m, i], tr.at[m, i], (at(x, zz, c), 1 - h, y),
            )

    def wait_less(m):
        for i, zz in enumerate([z] + zpeers):
            arrived(grem.at[:, zrows(m, zz), cols(m)], tr.at[m, i], ts.at[m, i])

    def transform(m):
        for a in range(3):
            for i in range(7):
                xx, cc = xpeers[opposite[i]]
                arrived(tile.at[m, a, xx * 2 + cc], xr.at[m, a, i], xs.at[m, a, i])
        for a in range(3):
            for k2 in range(8):
                j, cc = k2 // 2, k2 % 2
                values = [(tile[m, a, 2 * xx + cc, j, 0], tile[m, a, 2 * xx + cc, j, 1]) for xx in range(4)]
                for r1, value in enumerate(dft(values, 1)):
                    mid[a, r1, k2, 0], mid[a, r1, k2, 1] = cmul(value, k2 * r1)
        for r1 in range(4):
            sides = [dft([(mid[a, r1, k2, 0], mid[a, r1, k2, 1]) for k2 in range(8)], 1) for a in range(3)]
            out = []
            for (lr, li), (gr, gi), (wr, wi) in zip(*sides):
                ir = OUTER * wr + (OUTER * INNER) * (lr * gi - li * gr)
                ii = OUTER * wi + (OUTER * INNER) * (lr * gr + li * gi)
                out.append((-(lr * ii + li * ir), lr * ir - li * ii))
            for k2, value in enumerate(dft(out, -1)):
                mid2[r1, k2, 0], mid2[r1, k2, 1] = cmul(value, -k2 * r1)
        for k2 in range(8):
            j, cc = k2 // 2, k2 % 2
            for xx, value in enumerate(dft([(mid2[r1, k2, 0], mid2[r1, k2, 1]) for r1 in range(4)], -1)):
                sig[m, 2 * xx + cc, j, 0], sig[m, 2 * xx + cc, j, 1] = value
        for i, (xx, cc) in enumerate(xpeers):
            remote(
                sig.at[m, xx * 2 + cc], back.at[m, :, :, xrows(xc), :], bs.at[m, i], br.at[m, i], (at(xx, z, cc), h, y)
            )
        back[m, :, :, xrows(xc), :] = sig[m, xc]

    def back_z(m):
        for i in range(7):
            xx, cc = xpeers[opposite[i]]
            arrived(back.at[m, :, :, xrows(xx * 2 + cc), :], br.at[m, i], bs.at[m, i])
        for i, zz in enumerate(zpeers):
            remote(back.at[m, zz], sigma.at[y, m % 2, :, zrows(m, z), :], cs.at[m, i], cr.at[m, i], (at(x, zz, c), h, y))
        sigma[y, m % 2, :, zrows(m, z), :] = back[m, z]

    pieces = [z] + zpeers

    def piece(yy, m, i):
        return sigma.at[yy, m % 2, :, zrows(m, pieces[i]), :]

    def spread_y(m, i):
        if i > 0:
            arrived(piece(y, m, i), cr.at[m, i - 1], cs.at[m, i - 1])
        remote(piece(y, m, i), piece(y, m, i), ys.at[m, i, 0], yr.at[m, i, 0], (ka, h, up))
        remote(piece(y, m, i), piece(y, m, i), ys.at[m, i, 1], yr.at[m, i, 1], (ka, h, down))

    def relay_y(m, i):
        arrived(piece(down, m, i), yr.at[m, i, 0], ys.at[m, i, 0])
        if i % 2 == 0:
            remote(piece(down, m, i), piece(down, m, i), fs.at[m, i], fr.at[m, i], (ka, h, up))
        arrived(piece(up, m, i), yr.at[m, i, 1], ys.at[m, i, 1])
        if i % 2 == 1:
            remote(piece(up, m, i), piece(up, m, i), fs.at[m, i], fr.at[m, i], (ka, h, down))

    def wait_y(m):
        for i in range(4):
            arrived(piece((y + 2) % 4, m, i), fr.at[m, i], fs.at[m, i])

    def prepare(source, part, blocks):
        for s in blocks:
            re, im = source[0, s * 128:(s + 1) * 128, :], source[1, s * 128:(s + 1) * 128, :]
            for value, places in ((re, ((0, 0), (128, 256))), (im, ((0, 256),)), (-im, ((128, 0),))):
                high, low = split(value)
                for row, col in places:
                    ghigh[part * 4 + s, row:row + 128, col:col + 256] = high
                    glow[part * 4 + s, row:row + 128, col:col + 256] = low

    def multiply(m, part, first, last):
        def block(s, carry):
            multiply_one(m, part * 2 + s)
            return carry

        lax.fori_loop(first, last, block, 0)

    def multiply_one(m, yy):
        span = pl.ds((m // 2) * CROWS, CROWS)
        left = jnp.concatenate([sigma[yy, m % 2, 0, span, :], sigma[yy, m % 2, 1, span, :]], axis=1)
        high, low = split(left)
        index = yy * 2 + m % 2
        total = jnp.dot(high, ghigh[index], preferred_element_type=jnp.float32)
        total += jnp.dot(high, glow[index], preferred_element_type=jnp.float32)
        total += jnp.dot(low, ghigh[index], preferred_element_type=jnp.float32)
        acc[m // 2] += total

    results = []

    def finish(n):
        span = pl.ds(n * CROWS, CROWS)
        for ri in range(2):
            copy = pltpu.make_async_copy(
                acc.at[n, :, pl.ds(ri * 256, 256)], product.at[ri, 0, span, :], out_sem.at[n, ri]
            )
            copy.start()
            results.append(copy)

    for a in range(3):
        for m in range(CHUNKS):
            own[m][a].start()
    load.start()
    barrier = pltpu.get_barrier_semaphore()
    peers = [(at(x, zz, c), h, y) for zz in zpeers]
    peers += [(at(x, zz, c), 1 - h, y) for zz in range(4)]
    peers += [(at(xx, z, cc), h, y) for xx, cc in xpeers]
    peers += [(ka, h, up), (ka, h, down)]
    for peer in peers:
        pl.semaphore_signal(barrier, inc=1, device_id=peer, device_id_type=MESH)
    pl.semaphore_wait(barrier, len(peers))

    send_z(0, 0)
    send_z(0, 1)
    send_z(0, 2)
    send_z(1, 0)
    acc[...] = jnp.zeros_like(acc)
    load.wait()
    prepare(gloc, h, range(4))
    send_x(0, 0)
    send_z(1, 1)
    share_less(0)
    send_x(0, 1)
    send_z(1, 2)
    send_z(2, 0)
    send_x(0, 2)
    send_z(2, 1)
    send_x(1, 0)
    transform(0)
    send_x(1, 1)
    back_z(0)
    send_z(2, 2)
    share_less(1)
    send_x(1, 2)
    send_z(3, 0)
    send_x(2, 0)
    send_z(3, 1)
    transform(1)
    send_x(2, 1)
    back_z(1)
    send_z(3, 2)
    spread_y(0, 0)
    spread_y(0, 1)
    spread_y(0, 2)
    spread_y(0, 3)
    send_x(2, 2)
    relay_y(0, 0)
    relay_y(0, 1)
    relay_y(0, 2)
    relay_y(0, 3)
    send_x(3, 0)
    transform(2)
    spread_y(1, 0)
    spread_y(1, 1)
    spread_y(1, 2)
    spread_y(1, 3)
    send_x(3, 1)
    back_z(2)
    share_less(2)
    wait_y(0)
    multiply(0, h, 0, 2)
    send_x(3, 2)
    transform(3)
    relay_y(1, 0)
    relay_y(1, 1)
    relay_y(1, 2)
    relay_y(1, 3)
    spread_y(2, 0)
    spread_y(2, 1)
    spread_y(2, 2)
    spread_y(2, 3)
    back_z(3)
    share_less(3)
    wait_less(0)
    wait_less(1)
    prepare(grem, 1 - h, range(0, 2))
    wait_y(1)
    multiply(1, h, 0, 2)
    multiply(0, 1 - h, 0, 1)
    multiply(1, 1 - h, 0, 1)
    relay_y(2, 0)
    relay_y(2, 1)
    relay_y(2, 2)
    relay_y(2, 3)
    spread_y(3, 0)
    spread_y(3, 1)
    spread_y(3, 2)
    spread_y(3, 3)
    relay_y(3, 0)
    wait_y(2)
    multiply(2, h, 0, 2)
    multiply(2, 1 - h, 0, 1)
    relay_y(3, 1)
    relay_y(3, 2)
    relay_y(3, 3)
    wait_less(2)
    wait_less(3)
    prepare(grem, 1 - h, range(2, 4))
    multiply(0, 1 - h, 1, 2)
    multiply(1, 1 - h, 1, 2)
    finish(0)
    multiply(2, 1 - h, 1, 2)
    multiply_one(3, y)
    multiply_one(3, up)
    multiply_one(3, down)
    wait_y(3)
    multiply_one(3, (y + 2) % 4)
    finish(1)
    for copy in results:
        copy.wait()
    for copy in pending:
        copy.wait_send()


def body(green_less, green_great, screened):
    dma = pltpu.SemaphoreType.DMA
    block = jax.ShapeDtypeStruct(green_less.shape, jnp.float32)
    f32, bf16 = jnp.float32, jnp.bfloat16
    product = pl.pallas_call(
        kernel,
        out_shape=block,
        in_specs=[pl.BlockSpec(memory_space=pl.ANY)] * 3,
        out_specs=pl.BlockSpec(memory_space=pl.ANY),
        scratch_shapes=[
            pltpu.VMEM((CHUNKS, 3, 4, 2, ZROWS, CCOLS), f32),
            pltpu.VMEM((CHUNKS, 3, 8, 4, 2, TROWS, CCOLS), f32),
            pltpu.VMEM((3, 4, 8, 2, TROWS, CCOLS), f32),
            pltpu.VMEM((4, 8, 2, TROWS, CCOLS), f32),
            pltpu.VMEM((CHUNKS, 8, 4, 2, TROWS, CCOLS), f32),
            pltpu.VMEM((CHUNKS, 4, 2, ZROWS, CCOLS), f32),
            pltpu.VMEM((4, 2, 2, ROWS, CCOLS), f32),
            pltpu.VMEM((2, ROWS, COLS), f32),
            pltpu.VMEM((2, ROWS, COLS), f32),
            pltpu.VMEM((8, 256, 512), bf16),
            pltpu.VMEM((8, 256, 512), bf16),
            pltpu.VMEM((2, CROWS, 512), f32),
            dma((1 + 3 * CHUNKS,)), dma((2, 2)),
            dma((CHUNKS, 3, 3)), dma((CHUNKS, 3, 3)),
            dma((CHUNKS, 3, 7)), dma((CHUNKS, 3, 7)),
            dma((CHUNKS, 4)), dma((CHUNKS, 4)),
            dma((CHUNKS, 7)), dma((CHUNKS, 7)),
            dma((CHUNKS, 3)), dma((CHUNKS, 3)),
            dma((CHUNKS, 4, 2)), dma((CHUNKS, 4, 2)),
            dma((CHUNKS, 4)), dma((CHUNKS, 4)),
        ],
        compiler_params=pltpu.CompilerParams(collective_id=0, has_side_effects=True, vmem_limit_bytes=56 << 20),
        name="collide",
    )(green_less, green_great, screened)
    collision = product * NORM
    return collision, green_less + collision


def solution(mesh):
    spec = P(None, "ka", "tr", "tc")
    return jax.shard_map(body, mesh=mesh, in_specs=(spec,) * 3, out_specs=(spec,) * 2, check_vma=False)
```

time: 153 us -> 141 us (0.922); the launches traced: 153 us -> 139 us
  Pallas kernels: 149 us -> 135 us
  local copies, waits for them, and re-layouts: 3.32 us -> 0.01 us
  other arithmetic: 0 us -> 2.69 us
    pallas_call x1, Pallas kernels: 149 us -> 135 us  [body(): pl.pallas_call(kernel, out_shape=block, in_specs=[pl.BlockSpec(memory_spa...]
    unnamed x4 -> x2, local copies, waits for them, and re-layouts: 3.32 us -> 0.01 us
    add x0 -> x1, other arithmetic: none -> 2.69 us  [body(): return (collision, green_less + collision)]
where the time goes in v2:
time: 141 us; the launch traced here: 139 us
  Pallas kernels  135 us (96%)
  other arithmetic  2.69 us (2%)
    pallas_call x1, Pallas kernels, body(): pl.pallas_call(kernel, out_shape=block, in_specs=[pl.BlockSpec(memory_spa...  135 us

profile of v2, /device:TPU:1, one launch (start us, length us, event | category | flops | bytes accessed | tf_op | source)
XLA Modules:
  0.0 138.8 jit_solution(14321658654981057991)
XLA Ops:
  0.6 0.0 copy-start
  0.6 135.4 %collide.1 = f32[2,1,512,256]{3,2,1,0:T(8,128)} custom-call(f32[2,1,512,256]{3,2,1,0:T(8,128)} %less.1, f32[2,1,512,256]{3,2,1,0:T(8,128)} %great.1, f32[2,1,512,256]{3,2,1,0:T(8,128)} %screen.1), custom_call_target="tpu_custom_call" | custom-call | tf_op jit(solution)/shard_map/collide/pallas_call | solution.py:385
  136.1 0.0 copy-done
  136.1 2.7 %fusion = (f32[2,1,512,256]{3,2,1,0:T(8,128)}, f32[2,1,512,256]{3,2,1,0:T(8,128)}) fusion(f32[2,1,512,256]{3,2,1,0:T(8,128)S(1)} %copy-done, f32[2,1,512,256]{3,2,1,0:T(8,128)} %collide.1), kind=kLoop, calls=%fused_computation.1 | loop fusion | flops 524288 | bytes 4194304 | tf_op jit(solution)/shard_map/add | solution.py:416
Async XLA Ops:
  0.6 135.5 %copy-start = (f32[2,1,512,256]{3,2,1,0:T(8,128)S(1)}, f32[2,1,512,256]{3,2,1,0:T(8,128)}, u32[]{:S(2)}) copy-start(f32[2,1,512,256]{3,2,1,0:T(8,128)} %less.1) | copy-start | bytes 3145732

commit v3 on v2

--- a/solution.py
+++ b/solution.py
@@ -140,22 +140,10 @@
             )
         tile[m, a, xc] = zbuf[m, a, :, :, xrows(xc), :]
 
-    def arrive_z(m, a):
-        own[m][a].wait()
-        for i, zz in enumerate(zpeers):
-            arrived(zbuf.at[m, a, zz], zr.at[m, a, i], zs.at[m, a, i])
-
-    def arrive_x(m, a):
-        for i in range(7):
-            xx, cc = xpeers[opposite[i]]
-            arrived(tile.at[m, a, xx * 2 + cc], xr.at[m, a, i], xs.at[m, a, i])
-
-    def arrive_c(m):
-        for i, zz in enumerate(zpeers):
-            arrived(sigma.at[y, m % 2, :, zrows(m, zz), :], cr.at[m, i], cs.at[m, i])
-
-    def share_less(m):
+    def share_less(m, places):
         for i, zz in enumerate([z] + zpeers):
+            if i not in places:
+                continue
             remote(
                 zbuf.at[m, 0, zz], grem.at[:, zrows(m, z), cols(m)],
                 ts.at[m, i], tr.at[m, i], (at(x, zz, c), 1 - h, y),
@@ -285,80 +273,84 @@
     prepare(gloc, h, range(4))
     send_x(0, 0)
     send_z(1, 1)
-    share_less(0)
+    share_less(0, (1, 2))
     send_x(0, 1)
     send_z(1, 2)
+    send_x(0, 2)
     send_z(2, 0)
-    send_x(0, 2)
+    send_x(1, 0)
+    share_less(1, (1, 2))
     send_z(2, 1)
-    send_x(1, 0)
     transform(0)
     send_x(1, 1)
+    send_z(2, 2)
     back_z(0)
-    send_z(2, 2)
-    share_less(1)
     send_x(1, 2)
     send_z(3, 0)
     send_x(2, 0)
+    share_less(2, (1, 2))
     send_z(3, 1)
     transform(1)
     send_x(2, 1)
+    send_z(3, 2)
     back_z(1)
-    send_z(3, 2)
+    send_x(2, 2)
     spread_y(0, 0)
+    spread_y(0, 3)
     spread_y(0, 1)
     spread_y(0, 2)
-    spread_y(0, 3)
-    send_x(2, 2)
+    send_x(3, 0)
+    share_less(3, (1, 2))
+    share_less(0, (0, 3))
+    transform(2)
+    send_x(3, 1)
     relay_y(0, 0)
+    relay_y(0, 3)
     relay_y(0, 1)
     relay_y(0, 2)
-    relay_y(0, 3)
-    send_x(3, 0)
-    transform(2)
+    back_z(2)
+    send_x(3, 2)
+    share_less(1, (0, 3))
+    transform(3)
     spread_y(1, 0)
+    spread_y(1, 3)
     spread_y(1, 1)
     spread_y(1, 2)
-    spread_y(1, 3)
-    send_x(3, 1)
-    back_z(2)
-    share_less(2)
     wait_y(0)
     multiply(0, h, 0, 2)
-    send_x(3, 2)
-    transform(3)
+    back_z(3)
+    spread_y(2, 0)
     relay_y(1, 0)
+    relay_y(1, 3)
+    spread_y(2, 3)
     relay_y(1, 1)
     relay_y(1, 2)
-    relay_y(1, 3)
-    spread_y(2, 0)
     spread_y(2, 1)
     spread_y(2, 2)
-    spread_y(2, 3)
-    back_z(3)
-    share_less(3)
+    spread_y(3, 0)
+    relay_y(2, 0)
+    relay_y(2, 3)
+    spread_y(3, 3)
+    relay_y(2, 1)
+    spread_y(3, 1)
+    share_less(2, (0, 3))
+    share_less(3, (0, 3))
+    relay_y(2, 2)
+    spread_y(3, 2)
+    wait_y(1)
+    multiply(1, h, 0, 2)
     wait_less(0)
     wait_less(1)
     prepare(grem, 1 - h, range(0, 2))
-    wait_y(1)
-    multiply(1, h, 0, 2)
     multiply(0, 1 - h, 0, 1)
     multiply(1, 1 - h, 0, 1)
-    relay_y(2, 0)
-    relay_y(2, 1)
-    relay_y(2, 2)
-    relay_y(2, 3)
-    spread_y(3, 0)
-    spread_y(3, 1)
-    spread_y(3, 2)
-    spread_y(3, 3)
     relay_y(3, 0)
+    relay_y(3, 3)
+    relay_y(3, 1)
+    relay_y(3, 2)
     wait_y(2)
     multiply(2, h, 0, 2)
     multiply(2, 1 - h, 0, 1)
-    relay_y(3, 1)
-    relay_y(3, 2)
-    relay_y(3, 3)
     wait_less(2)
     wait_less(3)
     prepare(grem, 1 - h, range(2, 4))
@@ -409,7 +401,7 @@
             dma((CHUNKS, 4, 2)), dma((CHUNKS, 4, 2)),
             dma((CHUNKS, 4)), dma((CHUNKS, 4)),
         ],
-        compiler_params=pltpu.CompilerParams(collective_id=0, has_side_effects=True, vmem_limit_bytes=56 << 20),
+        compiler_params=pltpu.CompilerParams(collective_id=0, has_side_effects=True, vmem_limit_bytes=52 << 20),
         name="collide",
     )(green_less, green_great, screened)
     collision = product * NORM

time: 141 us -> 133 us (0.943); the launches traced: 139 us -> 133 us
  Pallas kernels: 135 us -> 131 us
    pallas_call x1, Pallas kernels: 135 us -> 131 us  [body(): pl.pallas_call(kernel, out_shape=block, in_specs=[pl.BlockSpec(memory_spa...]
where the time goes in v3:
time: 133 us
  Pallas kernels  131 us (98%)
  other arithmetic  1.47 us (1%)
    pallas_call x1, Pallas kernels, body(): pl.pallas_call(kernel, out_shape=block, in_specs=[pl.BlockSpec(memory_spa...  131 us

profile of v3, /device:TPU:1, one launch (start us, length us, event | category | flops | bytes accessed | tf_op | source)
XLA Modules:
  0.0 132.7 jit_solution(7679824782902043619)
XLA Ops:
  0.6 0.0 copy-start
  0.6 130.5 %collide.1 = f32[2,1,512,256]{3,2,1,0:T(8,128)S(1)} custom-call(f32[2,1,512,256]{3,2,1,0:T(8,128)} %less.1, f32[2,1,512,256]{3,2,1,0:T(8,128)} %great.1, f32[2,1,512,256]{3,2,1,0:T(8,128)} %screen.1), custom_call_target="tpu_custom_call" | custom-call | tf_op jit(solution)/shard_map/collide/pallas_call | solution.py:377
  131.2 0.0 copy-done
  131.2 1.5 %fusion = (f32[2,1,512,256]{3,2,1,0:T(8,128)}, f32[2,1,512,256]{3,2,1,0:T(8,128)}) fusion(f32[2,1,512,256]{3,2,1,0:T(8,128)S(1)} %copy-done, f32[2,1,512,256]{3,2,1,0:T(8,128)S(1)} %collide.1), kind=kLoop, calls=%fused_computation.1 | loop fusion | flops 524288 | bytes 4194304 | tf_op jit(solution)/shard_map/add | solution.py:408
Async XLA Ops:
  0.6 130.6 %copy-start = (f32[2,1,512,256]{3,2,1,0:T(8,128)S(1)}, f32[2,1,512,256]{3,2,1,0:T(8,128)}, u32[]{:S(2)}) copy-start(f32[2,1,512,256]{3,2,1,0:T(8,128)} %less.1) | copy-start | bytes 3145732

commit v4 on v3

--- a/solution.py
+++ b/solution.py
@@ -69,24 +69,22 @@
 
 def kernel(
     less, great, screen, product,
-    zbuf, tile, mid, mid2, sig, back, sigma, gloc, grem, ghigh, glow, acc,
-    own_sem, out_sem, zs, zr, xs, xr, ts, tr, bs, br, cs, cr, ys, yr, fs, fr,
+    zbuf, tile, mid, mid2, sig, back, sigma, gloc, grem, ghigh, glow,
+    own_sem, zs, zr, xs, xr, ts, tr, bs, br, cs, cr, ys, yr, fs, fr,
 ):
     ka, h, y = lax.axis_index("ka"), lax.axis_index("tr"), lax.axis_index("tc")
     x, z, c = ka // 8, (ka // 2) % 4, ka % 2
     xc = x * 2 + c
     arrays = (less, great, screen)
-    pending = []
 
     def at(xx, zz, cc):
         return xx * 8 + zz * 2 + cc
 
     zpeers = [3 - z, (z + 2) % 4, z + 1 - 2 * (z % 2)]
     xpeers = [
-        ((x + 1) % 4, c), ((x + 3) % 4, 1 - c), ((x + 1) % 4, 1 - c), ((x + 3) % 4, c),
-        ((x + 2) % 4, c), ((x + 2) % 4, 1 - c), (x, 1 - c),
+        ((x + 2) % 4, c), ((x + 2) % 4, 1 - c), ((x + 1) % 4, c), ((x + 3) % 4, 1 - c),
+        ((x + 1) % 4, 1 - c), ((x + 3) % 4, c), (x, 1 - c),
     ]
-    opposite = [3, 2, 1, 0, 4, 5, 6]
     up, down = (y + 1) % 4, (y + 3) % 4
 
     def remote(src, dst, send, recv, peer):
@@ -94,12 +92,21 @@
             src_ref=src, dst_ref=dst, send_sem=send, recv_sem=recv, device_id=peer, device_id_type=MESH
         )
         copy.start()
-        pending.append(copy)
-
-    def arrived(ref, sem, send):
-        pltpu.make_async_remote_copy(
-            src_ref=ref, dst_ref=ref, send_sem=send, recv_sem=sem, device_id=(ka, h, y), device_id_type=MESH
-        ).wait_recv()
+
+    def done(ref, sem):
+        pltpu.make_async_copy(ref, ref, sem).wait()
+
+    def three(m, a=0):
+        return zbuf.at[m, a, pl.ds(0, 3)]
+
+    def four(m):
+        return zbuf.at[m, 0]
+
+    def eight(m):
+        return zbuf.at[m, pl.ds(0, 2)]
+
+    def seven(m, a=0):
+        return tile.at[m, a, pl.ds(0, 7)]
 
     def rows(start, size):
         return pl.ds(pl.multiple_of(start, 8), size)
@@ -126,17 +133,16 @@
         for i, zz in enumerate(zpeers):
             remote(
                 arrays[a].at[:, 0, zrows(m, zz), cols(m)], zbuf.at[m, a, z],
-                zs.at[m, a, i], zr.at[m, a, i], (at(x, zz, c), h, y),
+                zs.at[m, a], zr.at[m, a], (at(x, zz, c), h, y),
             )
 
     def send_x(m, a):
         own[m][a].wait()
-        for i, zz in enumerate(zpeers):
-            arrived(zbuf.at[m, a, zz], zr.at[m, a, i], zs.at[m, a, i])
+        done(three(m, a), zr.at[m, a])
         for i, (xx, cc) in enumerate(xpeers):
             remote(
                 zbuf.at[m, a, :, :, xrows(xx * 2 + cc), :], tile.at[m, a, xc],
-                xs.at[m, a, i], xr.at[m, a, i], (at(xx, z, cc), h, y),
+                xs.at[m, a], xr.at[m, a], (at(xx, z, cc), h, y),
             )
         tile[m, a, xc] = zbuf[m, a, :, :, xrows(xc), :]
 
@@ -146,18 +152,15 @@
                 continue
             remote(
                 zbuf.at[m, 0, zz], grem.at[:, zrows(m, z), cols(m)],
-                ts.at[m, i], tr.at[m, i], (at(x, zz, c), 1 - h, y),
+                ts.at[m], tr.at[m], (at(x, zz, c), 1 - h, y),
             )
 
     def wait_less(m):
-        for i, zz in enumerate([z] + zpeers):
-            arrived(grem.at[:, zrows(m, zz), cols(m)], tr.at[m, i], ts.at[m, i])
+        done(four(m), tr.at[m])
 
     def transform(m):
         for a in range(3):
-            for i in range(7):
-                xx, cc = xpeers[opposite[i]]
-                arrived(tile.at[m, a, xx * 2 + cc], xr.at[m, a, i], xs.at[m, a, i])
+            done(seven(m, a), xr.at[m, a])
         for a in range(3):
             for k2 in range(8):
                 j, cc = k2 // 2, k2 % 2
@@ -179,16 +182,14 @@
                 sig[m, 2 * xx + cc, j, 0], sig[m, 2 * xx + cc, j, 1] = value
         for i, (xx, cc) in enumerate(xpeers):
             remote(
-                sig.at[m, xx * 2 + cc], back.at[m, :, :, xrows(xc), :], bs.at[m, i], br.at[m, i], (at(xx, z, cc), h, y)
+                sig.at[m, xx * 2 + cc], back.at[m, :, :, xrows(xc), :], bs.at[m], br.at[m], (at(xx, z, cc), h, y)
             )
         back[m, :, :, xrows(xc), :] = sig[m, xc]
 
     def back_z(m):
-        for i in range(7):
-            xx, cc = xpeers[opposite[i]]
-            arrived(back.at[m, :, :, xrows(xx * 2 + cc), :], br.at[m, i], bs.at[m, i])
+        done(seven(m), br.at[m])
         for i, zz in enumerate(zpeers):
-            remote(back.at[m, zz], sigma.at[y, m % 2, :, zrows(m, z), :], cs.at[m, i], cr.at[m, i], (at(x, zz, c), h, y))
+            remote(back.at[m, zz], sigma.at[y, m % 2, :, zrows(m, z), :], cs.at[m], cr.at[m, i], (at(x, zz, c), h, y))
         sigma[y, m % 2, :, zrows(m, z), :] = back[m, z]
 
     pieces = [z] + zpeers
@@ -198,21 +199,20 @@
 
     def spread_y(m, i):
         if i > 0:
-            arrived(piece(y, m, i), cr.at[m, i - 1], cs.at[m, i - 1])
-        remote(piece(y, m, i), piece(y, m, i), ys.at[m, i, 0], yr.at[m, i, 0], (ka, h, up))
-        remote(piece(y, m, i), piece(y, m, i), ys.at[m, i, 1], yr.at[m, i, 1], (ka, h, down))
+            done(piece(y, m, i), cr.at[m, i - 1])
+        remote(piece(y, m, i), piece(y, m, i), ys.at[m], yr.at[m, i, 0], (ka, h, up))
+        remote(piece(y, m, i), piece(y, m, i), ys.at[m], yr.at[m, i, 1], (ka, h, down))
 
     def relay_y(m, i):
-        arrived(piece(down, m, i), yr.at[m, i, 0], ys.at[m, i, 0])
+        done(piece(down, m, i), yr.at[m, i, 0])
         if i % 2 == 0:
-            remote(piece(down, m, i), piece(down, m, i), fs.at[m, i], fr.at[m, i], (ka, h, up))
-        arrived(piece(up, m, i), yr.at[m, i, 1], ys.at[m, i, 1])
+            remote(piece(down, m, i), piece(down, m, i), fs.at[m], fr.at[m], (ka, h, up))
+        done(piece(up, m, i), yr.at[m, i, 1])
         if i % 2 == 1:
-            remote(piece(up, m, i), piece(up, m, i), fs.at[m, i], fr.at[m, i], (ka, h, down))
+            remote(piece(up, m, i), piece(up, m, i), fs.at[m], fr.at[m], (ka, h, down))
 
     def wait_y(m):
-        for i in range(4):
-            arrived(piece((y + 2) % 4, m, i), fr.at[m, i], fs.at[m, i])
+        done(four(m), fr.at[m])
 
     def prepare(source, part, blocks):
         for s in blocks:
@@ -238,23 +238,12 @@
         total = jnp.dot(high, ghigh[index], preferred_element_type=jnp.float32)
         total += jnp.dot(high, glow[index], preferred_element_type=jnp.float32)
         total += jnp.dot(low, ghigh[index], preferred_element_type=jnp.float32)
-        acc[m // 2] += total
-
-    results = []
+        for ri in range(2):
+            product[ri, 0, span, :] += total[:, ri * 256:(ri + 1) * 256]
 
     def finish(n):
-        span = pl.ds(n * CROWS, CROWS)
-        for ri in range(2):
-            copy = pltpu.make_async_copy(
-                acc.at[n, :, pl.ds(ri * 256, 256)], product.at[ri, 0, span, :], out_sem.at[n, ri]
-            )
-            copy.start()
-            results.append(copy)
-
-    for a in range(3):
-        for m in range(CHUNKS):
-            own[m][a].start()
-    load.start()
+        del n
+
     barrier = pltpu.get_barrier_semaphore()
     peers = [(at(x, zz, c), h, y) for zz in zpeers]
     peers += [(at(x, zz, c), 1 - h, y) for zz in range(4)]
@@ -262,16 +251,20 @@
     peers += [(ka, h, up), (ka, h, down)]
     for peer in peers:
         pl.semaphore_signal(barrier, inc=1, device_id=peer, device_id_type=MESH)
+    for a in range(3):
+        for m in range(CHUNKS):
+            own[m][a].start()
+    load.start()
     pl.semaphore_wait(barrier, len(peers))
 
     send_z(0, 0)
     send_z(0, 1)
-    send_z(0, 2)
-    send_z(1, 0)
-    acc[...] = jnp.zeros_like(acc)
+    product[...] = jnp.zeros_like(product)
     load.wait()
     prepare(gloc, h, range(4))
+    send_z(0, 2)
     send_x(0, 0)
+    send_z(1, 0)
     send_z(1, 1)
     share_less(0, (1, 2))
     send_x(0, 1)
@@ -364,10 +357,15 @@
     wait_y(3)
     multiply_one(3, (y + 2) % 4)
     finish(1)
-    for copy in results:
-        copy.wait()
-    for copy in pending:
-        copy.wait_send()
+    for m in range(CHUNKS):
+        for a in range(3):
+            done(three(m, a), zs.at[m, a])
+            done(seven(m, a), xs.at[m, a])
+        done(four(m), ts.at[m])
+        done(seven(m), bs.at[m])
+        done(three(m), cs.at[m])
+        done(eight(m), ys.at[m])
+        done(four(m), fs.at[m])
 
 
 def body(green_less, green_great, screened):
@@ -378,7 +376,7 @@
         kernel,
         out_shape=block,
         in_specs=[pl.BlockSpec(memory_space=pl.ANY)] * 3,
-        out_specs=pl.BlockSpec(memory_space=pl.ANY),
+        out_specs=pl.BlockSpec(memory_space=pltpu.VMEM),
         scratch_shapes=[
             pltpu.VMEM((CHUNKS, 3, 4, 2, ZROWS, CCOLS), f32),
             pltpu.VMEM((CHUNKS, 3, 8, 4, 2, TROWS, CCOLS), f32),
@@ -391,15 +389,14 @@
             pltpu.VMEM((2, ROWS, COLS), f32),
             pltpu.VMEM((8, 256, 512), bf16),
             pltpu.VMEM((8, 256, 512), bf16),
-            pltpu.VMEM((2, CROWS, 512), f32),
-            dma((1 + 3 * CHUNKS,)), dma((2, 2)),
-            dma((CHUNKS, 3, 3)), dma((CHUNKS, 3, 3)),
-            dma((CHUNKS, 3, 7)), dma((CHUNKS, 3, 7)),
-            dma((CHUNKS, 4)), dma((CHUNKS, 4)),
-            dma((CHUNKS, 7)), dma((CHUNKS, 7)),
+            dma((1 + 3 * CHUNKS,)),
             dma((CHUNKS, 3)), dma((CHUNKS, 3)),
-            dma((CHUNKS, 4, 2)), dma((CHUNKS, 4, 2)),
-            dma((CHUNKS, 4)), dma((CHUNKS, 4)),
+            dma((CHUNKS, 3)), dma((CHUNKS, 3)),
+            dma((CHUNKS,)), dma((CHUNKS,)),
+            dma((CHUNKS,)), dma((CHUNKS,)),
+            dma((CHUNKS,)), dma((CHUNKS, 3)),
+            dma((CHUNKS,)), dma((CHUNKS, 4, 2)),
+            dma((CHUNKS,)), dma((CHUNKS,)),
         ],
         compiler_params=pltpu.CompilerParams(collective_id=0, has_side_effects=True, vmem_limit_bytes=52 << 20),
         name="collide",

time: 133 us -> 130 us (0.977); the launches traced: 133 us -> 128 us
  Pallas kernels: 131 us -> 126 us
    pallas_call x1, Pallas kernels: 131 us -> 126 us  [body(): pl.pallas_call(kernel, out_shape=block, in_specs=[pl.BlockSpec(memory_spa...]
where the time goes in v4:
time: 130 us; the launch traced here: 128 us
  Pallas kernels  126 us (97%)
  other arithmetic  1.47 us (1%)
    pallas_call x1, Pallas kernels, body(): pl.pallas_call(kernel, out_shape=block, in_specs=[pl.BlockSpec(memory_spa...  126 us

profile of v4, /device:TPU:1, one launch (start us, length us, event | category | flops | bytes accessed | tf_op | source)
XLA Modules:
  0.0 128.3 jit_solution(397462027468633856)
XLA Ops:
  0.6 0.0 copy-start
  0.6 126.1 %collide.1 = f32[2,1,512,256]{3,2,1,0:T(8,128)S(1)} custom-call(f32[2,1,512,256]{3,2,1,0:T(8,128)} %less.1, f32[2,1,512,256]{3,2,1,0:T(8,128)} %great.1, f32[2,1,512,256]{3,2,1,0:T(8,128)} %screen.1), custom_call_target="tpu_custom_call" | custom-call | tf_op jit(solution)/shard_map/collide/pallas_call | solution.py:375
  126.8 0.0 copy-done
  126.8 1.5 %fusion = (f32[2,1,512,256]{3,2,1,0:T(8,128)}, f32[2,1,512,256]{3,2,1,0:T(8,128)}) fusion(f32[2,1,512,256]{3,2,1,0:T(8,128)S(1)} %copy-done, f32[2,1,512,256]{3,2,1,0:T(8,128)S(1)} %collide.1), kind=kLoop, calls=%fused_computation.1 | loop fusion | flops 524288 | bytes 4194304 | tf_op jit(solution)/shard_map/add | solution.py:405
Async XLA Ops:
  0.6 126.2 %copy-start = (f32[2,1,512,256]{3,2,1,0:T(8,128)S(1)}, f32[2,1,512,256]{3,2,1,0:T(8,128)}, u32[]{:S(2)}) copy-start(f32[2,1,512,256]{3,2,1,0:T(8,128)} %less.1) | copy-start | bytes 3145732

commit v5 on v4

--- a/solution.py
+++ b/solution.py
@@ -70,7 +70,7 @@
 def kernel(
     less, great, screen, product,
     zbuf, tile, mid, mid2, sig, back, sigma, gloc, grem, ghigh, glow,
-    own_sem, zs, zr, xs, xr, ts, tr, bs, br, cs, cr, ys, yr, fs, fr,
+    own_sem, zs, zr, xr, tr, br, cr, yr, yn, fr,
 ):
     ka, h, y = lax.axis_index("ka"), lax.axis_index("tr"), lax.axis_index("tc")
     x, z, c = ka // 8, (ka // 2) % 4, ka % 2
@@ -122,7 +122,7 @@
 
     own = [
         [
-            pltpu.make_async_copy(arrays[a].at[:, 0, zrows(m, z), cols(m)], zbuf.at[m, a, z], own_sem.at[1 + 3 * m + a])
+            pltpu.make_async_copy(arrays[a].at[:, 0, zrows(m, z), cols(m)], zbuf.at[m, a, z], own_sem.at[1 + a])
             for a in range(3)
         ]
         for m in range(CHUNKS)
@@ -133,16 +133,17 @@
         for i, zz in enumerate(zpeers):
             remote(
                 arrays[a].at[:, 0, zrows(m, zz), cols(m)], zbuf.at[m, a, z],
-                zs.at[m, a], zr.at[m, a], (at(x, zz, c), h, y),
+                zs.at[0], zr.at[m, a], (at(x, zz, c), h, y),
             )
 
     def send_x(m, a):
-        own[m][a].wait()
+        if m == 0:
+            done(four(0), own_sem.at[1 + a])
         done(three(m, a), zr.at[m, a])
         for i, (xx, cc) in enumerate(xpeers):
             remote(
                 zbuf.at[m, a, :, :, xrows(xx * 2 + cc), :], tile.at[m, a, xc],
-                xs.at[m, a], xr.at[m, a], (at(xx, z, cc), h, y),
+                zs.at[1], xr.at[m, a], (at(xx, z, cc), h, y),
             )
         tile[m, a, xc] = zbuf[m, a, :, :, xrows(xc), :]
 
@@ -152,7 +153,7 @@
                 continue
             remote(
                 zbuf.at[m, 0, zz], grem.at[:, zrows(m, z), cols(m)],
-                ts.at[m], tr.at[m], (at(x, zz, c), 1 - h, y),
+                zs.at[2], tr.at[m], (at(x, zz, c), 1 - h, y),
             )
 
     def wait_less(m):
@@ -182,14 +183,14 @@
                 sig[m, 2 * xx + cc, j, 0], sig[m, 2 * xx + cc, j, 1] = value
         for i, (xx, cc) in enumerate(xpeers):
             remote(
-                sig.at[m, xx * 2 + cc], back.at[m, :, :, xrows(xc), :], bs.at[m], br.at[m], (at(xx, z, cc), h, y)
+                sig.at[m, xx * 2 + cc], back.at[m, :, :, xrows(xc), :], zs.at[3], br.at[m], (at(xx, z, cc), h, y)
             )
         back[m, :, :, xrows(xc), :] = sig[m, xc]
 
     def back_z(m):
         done(seven(m), br.at[m])
         for i, zz in enumerate(zpeers):
-            remote(back.at[m, zz], sigma.at[y, m % 2, :, zrows(m, z), :], cs.at[m], cr.at[m, i], (at(x, zz, c), h, y))
+            remote(back.at[m, zz], sigma.at[y, m % 2, :, zrows(m, z), :], zs.at[4], cr.at[m, i], (at(x, zz, c), h, y))
         sigma[y, m % 2, :, zrows(m, z), :] = back[m, z]
 
     pieces = [z] + zpeers
@@ -200,16 +201,17 @@
     def spread_y(m, i):
         if i > 0:
             done(piece(y, m, i), cr.at[m, i - 1])
-        remote(piece(y, m, i), piece(y, m, i), ys.at[m], yr.at[m, i, 0], (ka, h, up))
-        remote(piece(y, m, i), piece(y, m, i), ys.at[m], yr.at[m, i, 1], (ka, h, down))
+        ups = (yr.at[m, i], yn.at[m])
+        for peer, sem in (((ka, h, up), ups[i % 2]), ((ka, h, down), ups[1 - i % 2])):
+            remote(piece(y, m, i), piece(y, m, i), zs.at[5], sem, peer)
 
     def relay_y(m, i):
-        done(piece(down, m, i), yr.at[m, i, 0])
-        if i % 2 == 0:
-            remote(piece(down, m, i), piece(down, m, i), fs.at[m], fr.at[m], (ka, h, up))
-        done(piece(up, m, i), yr.at[m, i, 1])
-        if i % 2 == 1:
-            remote(piece(up, m, i), piece(up, m, i), fs.at[m], fr.at[m], (ka, h, down))
+        source, target = ((down, up), (up, down))[i % 2]
+        done(piece(source, m, i), yr.at[m, i])
+        remote(piece(source, m, i), piece(source, m, i), zs.at[6], fr.at[m], (ka, h, target))
+
+    def wait_near(m):
+        done(four(m), yn.at[m])
 
     def wait_y(m):
         done(four(m), fr.at[m])
@@ -240,9 +242,6 @@
         total += jnp.dot(low, ghigh[index], preferred_element_type=jnp.float32)
         for ri in range(2):
             product[ri, 0, span, :] += total[:, ri * 256:(ri + 1) * 256]
-
-    def finish(n):
-        del n
 
     barrier = pltpu.get_barrier_semaphore()
     peers = [(at(x, zz, c), h, y) for zz in zpeers]
@@ -309,6 +308,7 @@
     spread_y(1, 3)
     spread_y(1, 1)
     spread_y(1, 2)
+    wait_near(0)
     wait_y(0)
     multiply(0, h, 0, 2)
     back_z(3)
@@ -330,6 +330,7 @@
     share_less(3, (0, 3))
     relay_y(2, 2)
     spread_y(3, 2)
+    wait_near(1)
     wait_y(1)
     multiply(1, h, 0, 2)
     wait_less(0)
@@ -341,6 +342,7 @@
     relay_y(3, 3)
     relay_y(3, 1)
     relay_y(3, 2)
+    wait_near(2)
     wait_y(2)
     multiply(2, h, 0, 2)
     multiply(2, 1 - h, 0, 1)
@@ -349,23 +351,20 @@
     prepare(grem, 1 - h, range(2, 4))
     multiply(0, 1 - h, 1, 2)
     multiply(1, 1 - h, 1, 2)
-    finish(0)
     multiply(2, 1 - h, 1, 2)
+    wait_near(3)
     multiply_one(3, y)
     multiply_one(3, up)
     multiply_one(3, down)
     wait_y(3)
     multiply_one(3, (y + 2) % 4)
-    finish(1)
-    for m in range(CHUNKS):
-        for a in range(3):
-            done(three(m, a), zs.at[m, a])
-            done(seven(m, a), xs.at[m, a])
-        done(four(m), ts.at[m])
-        done(seven(m), bs.at[m])
-        done(three(m), cs.at[m])
-        done(eight(m), ys.at[m])
-        done(four(m), fs.at[m])
+    done(zbuf.at[:, :, pl.ds(0, 3)], zs.at[0])
+    done(tile.at[:, :, pl.ds(0, 7)], zs.at[1])
+    done(zbuf.at[:, 0], zs.at[2])
+    done(tile.at[:, 0, pl.ds(0, 7)], zs.at[3])
+    done(zbuf.at[:, 0, pl.ds(0, 3)], zs.at[4])
+    done(zbuf.at[:, pl.ds(0, 2)], zs.at[5])
+    done(zbuf.at[:, 0], zs.at[6])
 
 
 def body(green_less, green_great, screened):
@@ -389,14 +388,10 @@
             pltpu.VMEM((2, ROWS, COLS), f32),
             pltpu.VMEM((8, 256, 512), bf16),
             pltpu.VMEM((8, 256, 512), bf16),
-            dma((1 + 3 * CHUNKS,)),
+            dma((4,)), dma((7,)),
             dma((CHUNKS, 3)), dma((CHUNKS, 3)),
-            dma((CHUNKS, 3)), dma((CHUNKS, 3)),
-            dma((CHUNKS,)), dma((CHUNKS,)),
-            dma((CHUNKS,)), dma((CHUNKS,)),
-            dma((CHUNKS,)), dma((CHUNKS, 3)),
-            dma((CHUNKS,)), dma((CHUNKS, 4, 2)),
-            dma((CHUNKS,)), dma((CHUNKS,)),
+            dma((CHUNKS,)), dma((CHUNKS,)), dma((CHUNKS, 3)),
+            dma((CHUNKS, 4)), dma((CHUNKS,)), dma((CHUNKS,)),
         ],
         compiler_params=pltpu.CompilerParams(collective_id=0, has_side_effects=True, vmem_limit_bytes=52 << 20),
         name="collide",

time: 130 us -> 129 us (level)
  no operation moved by 1% of the time
where the time goes in v5:
time: 129 us; the launch traced here: 128 us
  Pallas kernels  126 us (98%)
  other arithmetic  1.47 us (1%)
    pallas_call x1, Pallas kernels, body(): pl.pallas_call(kernel, out_shape=block, in_specs=[pl.BlockSpec(memory_spa...  126 us

profile of v5, /device:TPU:1, one launch (start us, length us, event | category | flops | bytes accessed | tf_op | source)
XLA Modules:
  0.0 127.7 jit_solution(17586024509034680396)
XLA Ops:
  0.6 0.0 copy-start
  0.6 125.6 %collide.1 = f32[2,1,512,256]{3,2,1,0:T(8,128)S(1)} custom-call(f32[2,1,512,256]{3,2,1,0:T(8,128)} %less.1, f32[2,1,512,256]{3,2,1,0:T(8,128)} %great.1, f32[2,1,512,256]{3,2,1,0:T(8,128)} %screen.1), custom_call_target="tpu_custom_call" | custom-call | tf_op jit(solution)/shard_map/collide/pallas_call | solution.py:374
  126.3 0.0 copy-done
  126.3 1.5 %fusion = (f32[2,1,512,256]{3,2,1,0:T(8,128)}, f32[2,1,512,256]{3,2,1,0:T(8,128)}) fusion(f32[2,1,512,256]{3,2,1,0:T(8,128)S(1)} %copy-done, f32[2,1,512,256]{3,2,1,0:T(8,128)S(1)} %collide.1), kind=kLoop, calls=%fused_computation.1 | loop fusion | flops 524288 | bytes 4194304 | tf_op jit(solution)/shard_map/add | solution.py:400
Async XLA Ops:
  0.6 125.6 %copy-start = (f32[2,1,512,256]{3,2,1,0:T(8,128)S(1)}, f32[2,1,512,256]{3,2,1,0:T(8,128)}, u32[]{:S(2)}) copy-start(f32[2,1,512,256]{3,2,1,0:T(8,128)} %less.1) | copy-start | bytes 3145732

commit v6 on v5

--- a/solution.py
+++ b/solution.py
@@ -80,7 +80,7 @@
     def at(xx, zz, cc):
         return xx * 8 + zz * 2 + cc
 
-    zpeers = [3 - z, (z + 2) % 4, z + 1 - 2 * (z % 2)]
+    zpeers = [(z + 2) % 4, 3 - z, z + 1 - 2 * (z % 2)]
     xpeers = [
         ((x + 2) % 4, c), ((x + 2) % 4, 1 - c), ((x + 1) % 4, c), ((x + 3) % 4, 1 - c),
         ((x + 1) % 4, 1 - c), ((x + 3) % 4, c), (x, 1 - c),

time: 129 us -> 128 us (level)
  Pallas kernels: 126 us -> 124 us
where the time goes in v6:
time: 128 us; the launch traced here: 126 us
  Pallas kernels  124 us (97%)
  other arithmetic  1.47 us (1%)
    pallas_call x1, Pallas kernels, body(): pl.pallas_call(kernel, out_shape=block, in_specs=[pl.BlockSpec(memory_spa...  124 us

profile of v6, /device:TPU:1, one launch (start us, length us, event | category | flops | bytes accessed | tf_op | source)
XLA Modules:
  0.0 126.5 jit_solution(12590749521652014301)
XLA Ops:
  0.6 0.0 copy-start
  0.6 124.4 %collide.1 = f32[2,1,512,256]{3,2,1,0:T(8,128)S(1)} custom-call(f32[2,1,512,256]{3,2,1,0:T(8,128)} %less.1, f32[2,1,512,256]{3,2,1,0:T(8,128)} %great.1, f32[2,1,512,256]{3,2,1,0:T(8,128)} %screen.1), custom_call_target="tpu_custom_call" | custom-call | tf_op jit(solution)/shard_map/collide/pallas_call | solution.py:374
  125.0 0.0 copy-done
  125.0 1.5 %fusion = (f32[2,1,512,256]{3,2,1,0:T(8,128)}, f32[2,1,512,256]{3,2,1,0:T(8,128)}) fusion(f32[2,1,512,256]{3,2,1,0:T(8,128)S(1)} %copy-done, f32[2,1,512,256]{3,2,1,0:T(8,128)S(1)} %collide.1), kind=kLoop, calls=%fused_computation.1 | loop fusion | flops 524288 | bytes 4194304 | tf_op jit(solution)/shard_map/add | solution.py:400
Async XLA Ops:
  0.6 124.4 %copy-start = (f32[2,1,512,256]{3,2,1,0:T(8,128)S(1)}, f32[2,1,512,256]{3,2,1,0:T(8,128)}, u32[]{:S(2)}) copy-start(f32[2,1,512,256]{3,2,1,0:T(8,128)} %less.1) | copy-start | bytes 3145732
